TPU v7x, 32 devices: a whole 2x2x4 slice. The times are simulated.
32 devices in a mesh: grp: 4 (over z), term: 8 (over y, x, core).
Axes of the slice: x: 2, y: 2, z: 4, core: 2. Of those that a mesh axis runs over, the one named last changes fastest.
Arguments:
- hidden_states: bfloat16 [16384, 768], P(('grp', 'term')), may hold values from -8 to 8
- lengths: int32 [128], P(('grp', 'term')), may hold values from 32 to 128, as said below
- block_list: int32 [128, 96], P(('grp', 'term')), may hold values from 0 to 128, as said below
- cluster_ids: int32 [128], P(('grp', 'term')), may hold values from 0 to 16383, as said below
- attn_weight: bfloat16 [768, 2304], replicated, may hold values from -4 to 4
- out_weight: bfloat16 [768, 768], replicated, may hold values from -0.21875 to 0.21875
- up_weight: bfloat16 [768, 3072], replicated, may hold values from -0.21875 to 0.21875
- down_weight: bfloat16 [3072, 768], replicated, may hold values from -0.109375 to 0.109375
- head_weight: bfloat16 [768, 768], replicated, may hold values from -0.21875 to 0.21875
- head_gain: float32 [768], replicated, may hold values from 0.1 to 1.9
- vocab_weight: bfloat16 [16384, 768], P('term'), may hold values from -0.21875 to 0.21875
- vocab_bias: bfloat16 [16384], P('term'), may hold values from 0 to 2
- centroids: bfloat16 [16384, 768], P(('grp', 'term')), may hold values from -6 to 6
Outputs:
- sparse_weights: bfloat16 [128, 16384], P('grp', 'term')
- dense_slots: bfloat16 [32, 16, 768], P(('grp', 'term'))
- slot_passage: int32 [32, 16], P(('grp', 'term'))
Inputs may be any that keep to these rules, and one draw needn't show every extreme that they name: `lengths`: the first token of every passage is live; some passage has all 128 tokens live. `block_list`: the live entries of a row are distinct term blocks and come first; the rest equal 128, which names no block. Every row has at least 48 live entries and at least one padding entry. The 4 passages of one device have distinct owners (cluster_ids // 512). No owner has more than 16 passages, and some owner has exactly 16.
All inputs are finite; a program needn't handle non-finite values.
Results may differ from a plain program's by a relative error of at most 0.007.
Values may be sent and summed in bfloat16 or wider, within the bound.
A program may use at most 128 MiB of HBM per device.

v0:
```python
import functools
import math

import jax
import jax.numpy as jnp
from jax import lax
from jax.experimental import pallas as pl
from jax.experimental.pallas import tpu as pltpu
from jax.sharding import PartitionSpec as P

HEAD = 64
BLOCK = 128
CL_DEV = 512
CAP = 16
MESH = pl.DeviceIdType.MESH
F32 = jnp.float32
BF16 = jnp.bfloat16


def norm(values):
    center = values - jnp.mean(values, axis=-1, keepdims=True)
    spread = jnp.mean(center * center, axis=-1, keepdims=True)
    return center * lax.rsqrt(spread + 1e-06)


def gelu(v):
    return (0.5 * v) * (1.0 + lax.erf(v * math.sqrt(0.5)))


def mm(a, b):
    return jnp.dot(a, b, preferred_element_type=F32)


def mm_nt(a, b):
    return lax.dot_general(a, b, (((1,), (1,)), ((), ())), preferred_element_type=F32)


def kernel(
    groups,
    n,
    side,
    seq,
    chunk_passages,
    len_ref,
    hid_ref,
    gain_ref,
    meta_ref,
    aw_hbm,
    ow_hbm,
    uw_hbm,
    dw_hbm,
    hw_hbm,
    voc_hbm,
    pool_out,
    dall_out,
    aw,
    ow,
    uw,
    dw,
    hw,
    voc,
    gath,
    joined,
    ctx,
    fst,
    inner,
    dacc,
    payload,
    dall,
    pool,
    rpool,
    wsem,
    tok_send,
    tok_recv,
    d_send,
    d_recv,
    x_send,
    x_recv,
):
    grp = lax.axis_index("grp")
    term = lax.axis_index("term")
    devices = groups * n
    me = grp * n + term
    chips = n // 2
    chip = term // 2
    core = term % 2
    partner = {"grp": grp, "term": chip * 2 + (1 - core)}
    cy, cx = chip // side, chip % side
    width = hid_ref.shape[1]
    rows = chunk_passages * seq
    chunks = hid_ref.shape[0] // rows
    ff = uw.shape[1]
    relay = side == 2
    half = rows // 2

    def other(k):
        ky, kx = k // side, k % side
        to = ((cy + ky) % side) * side + (cx + kx) % side
        return {"grp": grp, "term": to * 2 + core}

    def source(k):
        ky, kx = k // side, k % side
        return ((cy + side - ky) % side) * side + (cx + side - kx) % side

    def everyone(d):
        to = (me + d) % devices
        return {"grp": to // n, "term": to % n}

    loads = [
        pltpu.make_async_copy(src, dst, wsem.at[i])
        for i, (src, dst) in enumerate(
            [(aw_hbm, aw), (ow_hbm, ow), (uw_hbm, uw), (dw_hbm, dw), (hw_hbm, hw), (voc_hbm, voc.at[0])]
        )
    ]
    for load in loads:
        load.start()

    barrier = pltpu.get_barrier_semaphore()

    @pl.loop(1, devices)
    def _(d):
        pl.semaphore_signal(barrier, inc=1, device_id=everyone(d), device_id_type=MESH)

    def tok_copy(h, k):
        return pltpu.make_async_remote_copy(
            src_ref=gath.at[0, h],
            dst_ref=gath.at[k, h],
            send_sem=tok_send.at[h, k],
            recv_sem=tok_recv.at[h, k],
            device_id=other(k),
            device_id_type=MESH,
        )

    def relay_copy(h, part):
        via = 1 + part
        span = pl.ds(part * half, half)
        return pltpu.make_async_remote_copy(
            src_ref=gath.at[via, h, span],
            dst_ref=gath.at[3, h, span],
            send_sem=tok_send.at[h, 3 + part],
            recv_sem=tok_recv.at[h, 3 + part],
            device_id=other(2 - part),
            device_id_type=MESH,
        )

    voc_copy = pltpu.make_async_remote_copy(
        src_ref=voc_hbm,
        dst_ref=voc.at[1],
        send_sem=x_send.at[0],
        recv_sem=x_recv.at[0],
        device_id=partner,
        device_id_type=MESH,
    )
    pool_copy = pltpu.make_async_remote_copy(
        src_ref=pool.at[1],
        dst_ref=rpool,
        send_sem=x_send.at[1],
        recv_sem=x_recv.at[1],
        device_id=partner,
        device_id_type=MESH,
    )

    def dense_copy(d):
        return pltpu.make_async_remote_copy(
            src_ref=payload,
            dst_ref=dall.at[me],
            send_sem=d_send.at[d],
            recv_sem=d_recv.at[d],
            device_id=everyone(d),
            device_id_type=MESH,
        )

    def send_direct(h):
        if relay:
            tok_copy(h, 1).start()
            tok_copy(h, 2).start()
        else:

            @pl.loop(1, chips)
            def _(k):
                tok_copy(h, k).start()

    def send_relay(h):
        if relay:
            for part in range(2):
                tok_copy(h, 1 + part).wait_recv()
                relay_copy(h, part).start()

    def first_wait(h, i):
        @pl.when(h == 0)
        def _():
            loads[i].wait()

    dacc[...] = meta_ref[...]
    pairs = width // (2 * HEAD)
    lane = lax.broadcasted_iota(jnp.int32, (seq, 2 * HEAD), 1)
    key_place = lax.broadcasted_iota(jnp.int32, (2 * seq, seq), 1)
    row_place = lax.broadcasted_iota(jnp.int32, (seq, width), 0)
    low = lane < HEAD

    def encode(h, carry):
        x = hid_ref[pl.ds(pl.multiple_of(h * rows, rows), rows), :]
        first_wait(h, 0)
        for c in range(3):
            cols = slice(c * width, (c + 1) * width)
            joined[:, cols] = mm(x, aw[:, cols]).astype(BF16)

        def attend(p, carry):
            span = pl.ds(pl.multiple_of(p * seq, seq), seq)
            live = key_place < len_ref[h * chunk_passages + p]
            for pair in range(pairs):
                at = pair * 2 * HEAD
                q = joined[span, at : at + 2 * HEAD]
                k = joined[span, width + at : width + at + 2 * HEAD]
                v = joined[span, 2 * width + at : 2 * width + at + 2 * HEAD]
                zero = jnp.zeros_like(q)
                both = jnp.concatenate([jnp.where(low, q, zero), jnp.where(low, zero, q)], axis=0)
                scores = mm_nt(both, k) * (1.0 / math.sqrt(HEAD))
                scores = jnp.where(live, scores, -1e30)
                expo = jnp.exp(scores - jnp.max(scores, axis=-1, keepdims=True))
                att = (expo * (1.0 / jnp.sum(expo, axis=-1, keepdims=True))).astype(BF16)
                mixed = mm(att, v)
                ctx[span, at : at + 2 * HEAD] = jnp.where(low, mixed[:seq], mixed[seq:]).astype(BF16)
            return carry

        lax.fori_loop(0, chunk_passages, attend, 0)
        first_wait(h, 1)
        fst[...] = norm(x.astype(F32) + mm(ctx[...], ow[...])).astype(BF16)
        first_wait(h, 2)
        tile = 512

        def up(j, carry):
            cols = pl.ds(pl.multiple_of(j * tile, tile), tile)
            inner[:, cols] = gelu(mm(fst[...], uw[:, cols])).astype(BF16)
            return carry

        lax.fori_loop(0, ff // tile, up, 0)
        first_wait(h, 3)
        layer_out = norm(fst[...].astype(F32) + mm(inner[...], dw[...])).astype(BF16)
        wide = layer_out.astype(F32)
        for p in range(chunk_passages):
            dacc[pl.ds(h * chunk_passages + p, 1), :] = wide[p * seq : p * seq + 1]
        first_wait(h, 4)
        out = norm(gelu(mm(layer_out, hw[...]))) * gain_ref[...]
        for p in range(chunk_passages):
            one = out[p * seq : (p + 1) * seq]
            one = jnp.where(row_place < len_ref[h * chunk_passages + p], one, one[0:1])
            gath[0, h, p * seq : (p + 1) * seq, :] = one.astype(BF16)

        @pl.when(h == 0)
        def _():
            pl.semaphore_wait(barrier, devices - 1)
            voc_copy.start()

        @pl.when(h > 0)
        def _():
            send_relay(h - 1)

        @pl.when(h == chunks - 1)
        def _():
            payload[...] = dacc[...].astype(BF16)

        send_direct(h)

        @pl.when(h == chunks - 1)
        def _():
            @pl.loop(1, devices)
            def _(d):
                dense_copy(d).start()

        return carry

    lax.fori_loop(0, chunks, encode, 0)
    loads[5].wait()
    voc_copy.wait_recv()

    terms = voc_hbm.shape[0]
    tile = min(512, terms)
    per_part = terms // tile

    def score(h, k):
        c = source(k)

        def step(j, carry):
            part, at = j // per_part, pl.multiple_of((j % per_part) * tile, tile)
            logits = mm_nt(gath[k, h], voc[part, pl.ds(at, tile), :])
            for p in range(chunk_passages):
                best = jnp.max(logits[p * seq : (p + 1) * seq], axis=0, keepdims=True)
                pool[part, c, h * chunk_passages + p, :, pl.ds(at, tile)] = best
            return carry

        lax.fori_loop(0, 2 * per_part, step, 0)

    for h in range(chunks):
        score(h, 0)
    for h in range(chunks):
        if relay:
            if h == chunks - 1:
                send_relay(h)
            score(h, 1)
            score(h, 2)
            relay_copy(h, 0).wait_recv()
            relay_copy(h, 1).wait_recv()
            score(h, 3)
        else:

            @pl.loop(1, chips)
            def _(k):
                tok_copy(h, k).wait_recv()
                score(h, k)

    pool_copy.start()
    dall[me] = payload[...]

    @pl.loop(1, devices)
    def _(d):
        dense_copy(d).wait_recv()

    dall_out[...] = dall[...]

    @pl.loop(0, chips)
    def _(c):
        pool_out[c, core] = pool[0, c]

    pool_copy.wait_recv()

    @pl.loop(0, chips)
    def _(c):
        pool_out[c, 1 - core] = rpool[c]

    pool_copy.wait_send()
    voc_copy.wait_send()

    @pl.loop(1, devices)
    def _(d):
        dense_copy(d).wait_send()

    for h in range(chunks):
        if relay:
            tok_copy(h, 1).wait_send()
            tok_copy(h, 2).wait_send()
            relay_copy(h, 0).wait_send()
            relay_copy(h, 1).wait_send()
        else:

            @pl.loop(1, chips)
            def _(k):
                tok_copy(h, k).wait_send()


def place_rows(rows, passage_ids, clusters, valid, centroids, device_id):
    valid_int = valid.astype(jnp.int32)
    ranks = jnp.cumsum(valid_int) - 1
    selected = valid[None, :] & (ranks[None, :] == jnp.arange(CAP, dtype=jnp.int32)[:, None])
    picked = jnp.dot(selected.astype(BF16), rows, preferred_element_type=F32)
    selected_int = selected.astype(jnp.int32)
    filled = jnp.sum(selected_int, axis=1) > 0
    picked_passage = jnp.sum(selected_int * passage_ids[None, :], axis=1)
    local_ids = clusters - device_id * CL_DEV
    picked_local = jnp.sum(selected_int * local_ids[None, :], axis=1)
    lookup = (picked_local[:, None] == jnp.arange(CL_DEV, dtype=jnp.int32)[None, :]) & filled[
        :, None
    ]
    chosen = jnp.dot(lookup.astype(BF16), centroids, preferred_element_type=F32)
    residual = (picked - chosen).astype(BF16)
    dense_part = jnp.where(filled[:, None], residual, jnp.zeros((), BF16))
    slot_part = jnp.where(filled, picked_passage, -1).astype(jnp.int32)
    return (dense_part, slot_part)


def body(
    groups,
    n,
    hidden,
    lengths,
    block_list,
    cluster_ids,
    attn_weight,
    out_weight,
    up_weight,
    down_weight,
    head_weight,
    head_gain,
    vocab_weight,
    vocab_bias,
    centroids,
):
    passages = lengths.shape[0]
    tokens, width = hidden.shape
    seq = tokens // passages
    ff = up_weight.shape[1]
    terms = vocab_weight.shape[0]
    devices = groups * n
    chips = n // 2
    side = math.isqrt(chips)
    chunk_passages = 2
    chunks = passages // chunk_passages
    rows = chunk_passages * seq
    grp = lax.axis_index("grp")
    term = lax.axis_index("term")
    me = grp * n + term
    blocks = n * terms // BLOCK
    listed = jnp.any(
        block_list[:, :, None] == jnp.arange(blocks, dtype=jnp.int32)[None, None, :], axis=1
    )
    marks = jnp.concatenate(
        [
            listed.astype(F32),
            (cluster_ids // 256).astype(F32)[:, None],
            (cluster_ids % 256).astype(F32)[:, None],
            jnp.zeros((passages, width - blocks - 2), F32),
        ],
        axis=1,
    )
    meta = jnp.concatenate([jnp.zeros((passages, width), F32), marks], axis=0)
    vm = pl.BlockSpec(memory_space=pltpu.VMEM)
    hbm = pl.BlockSpec(memory_space=pl.ANY)
    dma = pltpu.SemaphoreType.DMA
    pool, dall = pl.pallas_call(
        functools.partial(kernel, groups, n, side, seq, chunk_passages),
        out_shape=(
            jax.ShapeDtypeStruct((chips, 2, passages, 1, terms), F32),
            jax.ShapeDtypeStruct((devices, 2 * passages, width), BF16),
        ),
        in_specs=[pl.BlockSpec(memory_space=pltpu.SMEM), vm, vm, vm] + [hbm] * 6,
        out_specs=(vm, vm),
        scratch_shapes=[
            pltpu.VMEM(attn_weight.shape, BF16),
            pltpu.VMEM(out_weight.shape, BF16),
            pltpu.VMEM(up_weight.shape, BF16),
            pltpu.VMEM(down_weight.shape, BF16),
            pltpu.VMEM(head_weight.shape, BF16),
            pltpu.VMEM((2, terms, width), BF16),
            pltpu.VMEM((chips, chunks, rows, width), BF16),
            pltpu.VMEM((rows, 3 * width), BF16),
            pltpu.VMEM((rows, width), BF16),
            pltpu.VMEM((rows, width), BF16),
            pltpu.VMEM((rows, ff), BF16),
            pltpu.VMEM((2 * passages, width), F32),
            pltpu.VMEM((2 * passages, width), BF16),
            pltpu.VMEM((devices, 2 * passages, width), BF16),
            pltpu.VMEM((2, chips, passages, 1, terms), F32),
            pltpu.VMEM((chips, passages, 1, terms), F32),
            dma((6,)),
            dma((chunks, chips + 1)),
            dma((chunks, chips + 1)),
            dma((devices,)),
            dma((devices,)),
            dma((2,)),
            dma((2,)),
        ],
        compiler_params=pltpu.CompilerParams(
            collective_id=0, has_side_effects=True, vmem_limit_bytes=60 * 1024 * 1024
        ),
    )(
        lengths,
        hidden,
        head_gain[None, :],
        meta,
        attn_weight,
        out_weight,
        up_weight,
        down_weight,
        head_weight,
        vocab_weight,
    )
    raw = pool.reshape(n * passages, terms)
    mine = lax.dynamic_slice_in_dim(dall, grp * n, n, 0)[:, passages:]
    flags = lax.dynamic_slice_in_dim(mine, term * (terms // BLOCK), terms // BLOCK, 2)
    flags = flags.reshape(n * passages, terms // BLOCK)
    value = jnp.log1p(jax.nn.relu(raw + vocab_bias.astype(F32)[None, :]))
    keep = jnp.repeat(flags, BLOCK, axis=1) > 0.5
    sparse = jnp.where(keep, value, 0.0).astype(BF16)
    ids = dall[:, passages:, blocks : blocks + 2].astype(jnp.int32)
    clusters = (ids[:, :, 0] * 256 + ids[:, :, 1]).reshape(devices * passages)
    dense_rows = dall[:, :passages].reshape(devices * passages, width)
    dense_part, slot_part = place_rows(
        dense_rows,
        jnp.arange(devices * passages, dtype=jnp.int32),
        clusters,
        clusters // CL_DEV == me,
        centroids,
        me,
    )
    return (sparse, dense_part[None, :, :], slot_part[None, :])


def solution(mesh):
    placed = (
        P(("grp", "term"), None),
        P(("grp", "term")),
        P(("grp", "term"), None),
        P(("grp", "term")),
        P(),
        P(),
        P(),
        P(),
        P(),
        P(),
        P("term", None),
        P("term"),
        P(("grp", "term"), None),
    )
    return jax.shard_map(
        functools.partial(body, mesh.shape["grp"], mesh.shape["term"]),
        mesh=mesh,
        in_specs=placed,
        out_specs=(P("grp", "term"), P(("grp", "term"), None, None), P(("grp", "term"), None)),
        check_vma=False,
    )
```

profile of v0, /device:TPU:0, one launch (start us, length us, event | category | flops | bytes accessed | tf_op | source)
XLA Modules:
  0.0 68.1 jit_solution(15883735314467767890)
XLA Ops:
  0.6 0.0 copy-start
  0.6 1.3 %broadcast_in_dim.30.gain_ref = f32[1,768]{1,0:T(1,128)} reshape(f32[768]{0:T(1024)} %param.22) | data formatting | bytes 6144 | tf_op jit(solution)/shard_map/broadcast_in_dim | solution.py:458
  2.0 0.7 convert_bitcast_fusion
  2.7 0.1 copy.29
  2.7 0.1 copy.28
  2.8 0.8 %fusion.3 = pred[4,128]{1,0:T(4,128)(4,1)S(1)} fusion(s32[4,96]{1,0:T(4,128)} %param.15), kind=kLoop, calls=%fused_computation.6 | loop fusion | flops 97792 | bytes 2048 | tf_op jit(solution)/shard_map/reduce_or | solution.py:403
  3.7 0.1 pad.4.clone
  3.8 0.1 maximum_maximum_fusion
  3.8 0.6 concatenate.7.meta_ref
  4.4 0.0 copy-start.1
  4.5 55.3 %shard_map.148 = (f32[4,2,4,1,2048]{4,3,2,1,0:T(1,128)}, bf16[32,8,768]{2,1,0:T(8,128)(2,1)}) custom-call(s32[4]{0:T(128)} %len_ref.1, bf16[512,768]{1,0:T(8,128)(2,1)} %hid_ref.1, f32[1,768]{1,0:T(1,128)} %broadcast_in_dim.30.gain_ref, f32[8,768]{1,0:T(8,128)} %concatenate.7.meta_ref, bf16[768,2304]{1,0:T(8,128)(2,1)} %aw_hbm.1, bf16[768,768]{1,0:T(8,128)(2,1)} %ow_hbm.1, ...), custom_call_target="tpu_custom_call" | custom-call | tf_op jit(solution)/shard_map/pallas_call | solution.py:419
  59.8 1.6 %reduce = f32[4,2,4,2048]{3,2,1,0:T(4,128)S(1)} reduce(f32[4,2,4,1,2048]{4,3,2,1,0:T(1,128)} %get-tuple-element.6, f32[]{:T(128)} %constant.85), dimensions={3}, to_apply=%get-tuple-element.6.reduce_sub_computation | reduce | bytes 524292 | tf_op jit(solution)/shard_map/pallas_call | solution.py:419
  61.4 0.1 reshape.180
  61.5 0.8 %dynamic-slice_compare_fusion = pred[8,4,16]{2,1,0:T(4,128)(4,1)S(1)} fusion(bf16[32,8,768]{2,1,0:T(8,128)(2,1)} %get-tuple-element.5, s32[]{:T(128)S(6)} %select_n.62, s32[]{:T(128)S(6)} %add.84, s32[]{:T(128)S(6)} %select_n.63), kind=kLoop, calls=%fused_computation.25 | loop fusion | flops 1536 | bytes 1548 | tf_op jit(solution)/shard_map/gt | solution.py:472
  62.3 0.1 broadcast_in_dim.54
  62.4 0.0 copy-done.1
  62.5 0.8 %select_convert_fusion = bf16[32,2048]{1,0:T(8,128)(2,1)} fusion(f32[32,2048]{1,0:T(8,128)S(1)} %reshape.180, pred[4,8,16,128]{3,2,1,0:T(8,128)(4,1)S(1)} %bitcast.18, f32[2048]{0:T(1024)S(1)} %convert_element_type.41), kind=kLoop, calls=%fused_computation.4 | loop fusion | flops 262144 | bytes 466944 | tf_op jit(solution)/shard_map/convert_element_type | solution.py:473
  63.3 1.0 %slice.19 = bf16[32,4,768]{2,1,0:T(4,128)(2,1)S(1)} slice(bf16[32,8,768]{2,1,0:T(8,128)(2,1)} %get-tuple-element.5), slice={[0:32], [0:4], [0:768]} | slice | bytes 393216 | tf_op jit(solution)/shard_map/slice | solution.py:476
  64.3 0.1 reshape.181
  64.4 0.9 %slice_convert_fusion = s32[32,4,2]{2,1,0:T(4,128)S(1)} fusion(bf16[32,8,768]{2,1,0:T(8,128)(2,1)} %get-tuple-element.5), kind=kLoop, calls=%fused_computation.20 | loop fusion | flops 256 | bytes 1536 | tf_op jit(solution)/shard_map/convert_element_type | solution.py:474
  65.2 0.7 %fusion.20 = (s32[32,4]{1,0:T(8,128)S(1)}, s32[32,4,1]{2,1,0:T(4,128)S(1)}) fusion(s32[32,4,2]{2,1,0:T(4,128)S(1)} %slice_convert_fusion), kind=kLoop, calls=%fused_computation.50 | loop fusion | flops 256 | bytes 2048 | tf_op jit(solution)/shard_map/add | solution.py:475
  66.0 0.2 reduce-window.8
  66.2 0.1 add_reduce_fusion
  66.3 0.1 add.78
  66.4 0.1 fusion.13
  66.5 0.2 select_reduce_fusion
  66.7 0.0 copy-done
  66.7 0.9 %fusion.2 = bf16[1,16,768]{2,1,0:T(8,128)(2,1)} fusion(f32[16,768]{1,0:T(8,128)S(1)} %fusion.13, bf16[512,768]{1,0:T(8,128)(2,1)S(1)} %copy-done, pred[16]{0:T(512)(128)(4,1)S(1)} %broadcast_compare_fusion, s32[16]{0:T(128)S(1)} %get-tuple-element.8), kind=kOutput, calls=%fused_computation.3 | convolution fusion | flops 12636160 | bytes 860240 | tf_op jit(solution)/shard_map/dot_general | solution.py:364
  67.6 0.5 select_bitcast_fusion
  (7 shorter events, 0.1 us)
Async XLA Ops:
  0.6 66.1 %copy-start = (bf16[512,768]{1,0:T(8,128)(2,1)S(1)}, bf16[512,768]{1,0:T(8,128)(2,1)}, u32[]{:S(2)}) copy-start(bf16[512,768]{1,0:T(8,128)(2,1)} %param.25) | copy-start | bytes 2359300
  4.4 58.0 %copy-start.1 = (bf16[2048]{0:T(1024)(128)(2,1)S(1)}, bf16[2048]{0:T(1024)(128)(2,1)}, u32[]{:S(2)}) copy-start(bf16[2048]{0:T(1024)(128)(2,1)} %param.24) | copy-start | bytes 12292
where the time goes:
time: 68.5 us; the launch traced here: 68.1 us
  Pallas kernels  55.3 us (81%)
  other arithmetic  7.36 us (11%)
  local copies, waits for them, and re-layouts  3.67 us (5%)
  matrix products  1.01 us (1%)
  between operations  0.76 us (1%)
    pallas_call x1, Pallas kernels, body(): pl.pallas_call(functools.partial(kernel, groups, n, side, seq, chunk_pass...  55.3 us
    pallas_call x1, other arithmetic, body(): pl.pallas_call(functools.partial(kernel, groups, n, side, seq, chunk_pass...  1.64 us

commit v1 on v0

--- a/solution.py
+++ b/solution.py
@@ -42,22 +42,27 @@
     seq,
     chunk_passages,
     len_ref,
+    cid_ref,
     hid_ref,
     gain_ref,
-    meta_ref,
+    blk_ref,
+    bias_ref,
     aw_hbm,
     ow_hbm,
     uw_hbm,
     dw_hbm,
     hw_hbm,
     voc_hbm,
-    pool_out,
-    dall_out,
+    cen_hbm,
+    sparse_out,
+    dense_out,
+    slot_out,
     aw,
     ow,
     uw,
     dw,
     hw,
+    cen,
     voc,
     gath,
     joined,
@@ -68,7 +73,7 @@
     payload,
     dall,
     pool,
-    rpool,
+    res,
     wsem,
     tok_send,
     tok_recv,
@@ -109,7 +114,7 @@
     loads = [
         pltpu.make_async_copy(src, dst, wsem.at[i])
         for i, (src, dst) in enumerate(
-            [(aw_hbm, aw), (ow_hbm, ow), (uw_hbm, uw), (dw_hbm, dw), (hw_hbm, hw), (voc_hbm, voc.at[0])]
+            [(aw_hbm, aw), (ow_hbm, ow), (uw_hbm, uw), (dw_hbm, dw), (hw_hbm, hw), (voc_hbm, voc.at[0]), (cen_hbm, cen)]
         )
     ]
     for load in loads:
@@ -152,8 +157,8 @@
         device_id_type=MESH,
     )
     pool_copy = pltpu.make_async_remote_copy(
-        src_ref=pool.at[1],
-        dst_ref=rpool,
+        src_ref=pool,
+        dst_ref=res.at[core],
         send_sem=x_send.at[1],
         recv_sem=x_recv.at[1],
         device_id=partner,
@@ -191,7 +196,23 @@
         def _():
             loads[i].wait()
 
-    dacc[...] = meta_ref[...]
+    passages = len_ref.shape[0]
+    listing = blk_ref.shape[1]
+    blocks = n * voc_hbm.shape[0] // BLOCK
+    dacc[...] = jnp.zeros_like(dacc)
+    square = lax.broadcasted_iota(jnp.int32, (listing, listing), 0) == lax.broadcasted_iota(
+        jnp.int32, (listing, listing), 1
+    )
+    block_lane = lax.broadcasted_iota(jnp.int32, (listing, blocks), 1).astype(F32)
+    id_lane = lax.broadcasted_iota(jnp.int32, (1, 128), 1)
+    for p in range(passages):
+        line = blk_ref[p : p + 1, :].astype(F32)
+        column = jnp.sum(jnp.where(square, line, 0.0), axis=1, keepdims=True)
+        marks = jnp.max(jnp.where(column == block_lane, 1.0, 0.0), axis=0, keepdims=True)
+        dacc[passages + p : passages + p + 1, 0:blocks] = marks
+        cid = cid_ref[p]
+        ids = jnp.where(id_lane == 0, cid // 256, jnp.where(id_lane == 1, cid % 256, 0))
+        dacc[passages + p : passages + p + 1, blocks : blocks + 128] = ids.astype(F32)
     pairs = width // (2 * HEAD)
     lane = lax.broadcasted_iota(jnp.int32, (seq, 2 * HEAD), 1)
     key_place = lax.broadcasted_iota(jnp.int32, (2 * seq, seq), 1)
@@ -275,7 +296,7 @@
     voc_copy.wait_recv()
 
     terms = voc_hbm.shape[0]
-    tile = min(512, terms)
+    tile = min(1024, terms)
     per_part = terms // tile
 
     def score(h, k):
@@ -286,7 +307,15 @@
             logits = mm_nt(gath[k, h], voc[part, pl.ds(at, tile), :])
             for p in range(chunk_passages):
                 best = jnp.max(logits[p * seq : (p + 1) * seq], axis=0, keepdims=True)
-                pool[part, c, h * chunk_passages + p, :, pl.ds(at, tile)] = best
+                row = pl.ds(c * passages + h * chunk_passages + p, 1)
+
+                @pl.when(part == 0)
+                def _():
+                    res[core, row, pl.ds(at, tile)] = best
+
+                @pl.when(part == 1)
+                def _():
+                    pool[row, pl.ds(at, tile)] = best
             return carry
 
         lax.fori_loop(0, 2 * per_part, step, 0)
@@ -316,17 +345,59 @@
     def _(d):
         dense_copy(d).wait_recv()
 
-    dall_out[...] = dall[...]
-
-    @pl.loop(0, chips)
-    def _(c):
-        pool_out[c, core] = pool[0, c]
+    loads[6].wait()
+    span = 2 * passages
+    total = devices * span
+    flat = dall[...].astype(F32).reshape(total, width)
+    facts = flat[:, blocks : blocks + 128].astype(BF16)
+    pick = lax.broadcasted_iota(jnp.int32, (8, 128), 0) == lax.broadcasted_iota(
+        jnp.int32, (8, 128), 1
+    )
+    pieces = pltpu.roll(mm_nt(jnp.where(pick, 1.0, 0.0).astype(BF16), facts), total - passages, 1)
+    clusters = pieces[0:1] * 256.0 + pieces[1:2]
+    place = lax.broadcasted_iota(jnp.int32, (1, total), 1).astype(F32)
+    sender = jnp.floor(place / span)
+    within = place - sender * span
+    first = (me * CL_DEV).astype(F32)
+    local = clusters - first
+    own = (within < passages) & (local >= 0.0) & (local < CL_DEV)
+    own = jnp.where(own, 1.0, 0.0)
+    before = lax.broadcasted_iota(jnp.int32, (total, total), 0) < lax.broadcasted_iota(
+        jnp.int32, (total, total), 1
+    )
+    ranks = mm(
+        jnp.broadcast_to(own, (8, total)).astype(BF16), jnp.where(before, 1.0, 0.0).astype(BF16)
+    )[0:1]
+    slot = lax.broadcasted_iota(jnp.int32, (CAP, total), 0).astype(F32)
+    chosen = jnp.where((slot == ranks) & (own > 0.5), 1.0, 0.0)
+    filled = jnp.sum(chosen, axis=1, keepdims=True) > 0.5
+    passage = sender * passages + within
+    number = jnp.sum(chosen * (passage + 1.0), axis=1, keepdims=True) - 1.0
+    local = jnp.where(own > 0.5, local, 0.0)
+    entry = jnp.sum(chosen * local, axis=1, keepdims=True)
+    picked = mm(chosen.astype(BF16), flat.astype(BF16))
+    entries = lax.broadcasted_iota(jnp.int32, (CAP, CL_DEV), 1).astype(F32)
+    lookup = jnp.where((entries == entry) & filled, 1.0, 0.0).astype(BF16)
+    dense_out[0] = jnp.where(filled, picked - mm(lookup, cen[...]), 0.0).astype(BF16)
+    eye = lax.broadcasted_iota(jnp.int32, (CAP, CAP), 0) == lax.broadcasted_iota(
+        jnp.int32, (CAP, CAP), 1
+    )
+    slot_out[...] = jnp.sum(jnp.where(eye, number, 0.0), axis=0, keepdims=True).astype(jnp.int32)
+
+    peers = dall[pl.ds(grp * n, n), :, 0:blocks].astype(F32)
+    marks = jnp.concatenate([peers[t, passages:] for t in range(n)], axis=0).astype(BF16)
+    base = term * (terms // BLOCK)
+    offset = (lax.broadcasted_iota(jnp.int32, (blocks, terms), 0) - base) * BLOCK
+    column = lax.broadcasted_iota(jnp.int32, (blocks, terms), 1)
+    spread = jnp.where((column >= offset) & (column < offset + BLOCK), 1.0, 0.0).astype(BF16)
+    keep = mm(marks, spread) > 0.5
 
     pool_copy.wait_recv()
-
-    @pl.loop(0, chips)
-    def _(c):
-        pool_out[c, 1 - core] = rpool[c]
+    both = []
+    for c in range(chips):
+        both += [res[s, c * passages : (c + 1) * passages] for s in range(2)]
+    raw = jnp.concatenate(both, axis=0) + bias_ref[...].astype(F32)
+    sparse_out[...] = jnp.where(keep, jnp.log1p(jnp.maximum(raw, 0.0)), 0.0).astype(BF16)
 
     pool_copy.wait_send()
     voc_copy.wait_send()
@@ -346,26 +417,6 @@
             @pl.loop(1, chips)
             def _(k):
                 tok_copy(h, k).wait_send()
-
-
-def place_rows(rows, passage_ids, clusters, valid, centroids, device_id):
-    valid_int = valid.astype(jnp.int32)
-    ranks = jnp.cumsum(valid_int) - 1
-    selected = valid[None, :] & (ranks[None, :] == jnp.arange(CAP, dtype=jnp.int32)[:, None])
-    picked = jnp.dot(selected.astype(BF16), rows, preferred_element_type=F32)
-    selected_int = selected.astype(jnp.int32)
-    filled = jnp.sum(selected_int, axis=1) > 0
-    picked_passage = jnp.sum(selected_int * passage_ids[None, :], axis=1)
-    local_ids = clusters - device_id * CL_DEV
-    picked_local = jnp.sum(selected_int * local_ids[None, :], axis=1)
-    lookup = (picked_local[:, None] == jnp.arange(CL_DEV, dtype=jnp.int32)[None, :]) & filled[
-        :, None
-    ]
-    chosen = jnp.dot(lookup.astype(BF16), centroids, preferred_element_type=F32)
-    residual = (picked - chosen).astype(BF16)
-    dense_part = jnp.where(filled[:, None], residual, jnp.zeros((), BF16))
-    slot_part = jnp.where(filled, picked_passage, -1).astype(jnp.int32)
-    return (dense_part, slot_part)
 
 
 def body(
@@ -396,40 +447,25 @@
     chunk_passages = 2
     chunks = passages // chunk_passages
     rows = chunk_passages * seq
-    grp = lax.axis_index("grp")
-    term = lax.axis_index("term")
-    me = grp * n + term
-    blocks = n * terms // BLOCK
-    listed = jnp.any(
-        block_list[:, :, None] == jnp.arange(blocks, dtype=jnp.int32)[None, None, :], axis=1
-    )
-    marks = jnp.concatenate(
-        [
-            listed.astype(F32),
-            (cluster_ids // 256).astype(F32)[:, None],
-            (cluster_ids % 256).astype(F32)[:, None],
-            jnp.zeros((passages, width - blocks - 2), F32),
-        ],
-        axis=1,
-    )
-    meta = jnp.concatenate([jnp.zeros((passages, width), F32), marks], axis=0)
     vm = pl.BlockSpec(memory_space=pltpu.VMEM)
     hbm = pl.BlockSpec(memory_space=pl.ANY)
     dma = pltpu.SemaphoreType.DMA
-    pool, dall = pl.pallas_call(
+    return pl.pallas_call(
         functools.partial(kernel, groups, n, side, seq, chunk_passages),
         out_shape=(
-            jax.ShapeDtypeStruct((chips, 2, passages, 1, terms), F32),
-            jax.ShapeDtypeStruct((devices, 2 * passages, width), BF16),
+            jax.ShapeDtypeStruct((n * passages, terms), BF16),
+            jax.ShapeDtypeStruct((1, CAP, width), BF16),
+            jax.ShapeDtypeStruct((1, CAP), jnp.int32),
         ),
-        in_specs=[pl.BlockSpec(memory_space=pltpu.SMEM), vm, vm, vm] + [hbm] * 6,
-        out_specs=(vm, vm),
+        in_specs=[pl.BlockSpec(memory_space=pltpu.SMEM)] * 2 + [vm] * 4 + [hbm] * 7,
+        out_specs=(vm, vm, vm),
         scratch_shapes=[
             pltpu.VMEM(attn_weight.shape, BF16),
             pltpu.VMEM(out_weight.shape, BF16),
             pltpu.VMEM(up_weight.shape, BF16),
             pltpu.VMEM(down_weight.shape, BF16),
             pltpu.VMEM(head_weight.shape, BF16),
+            pltpu.VMEM(centroids.shape, BF16),
             pltpu.VMEM((2, terms, width), BF16),
             pltpu.VMEM((chips, chunks, rows, width), BF16),
             pltpu.VMEM((rows, 3 * width), BF16),
@@ -439,9 +475,9 @@
             pltpu.VMEM((2 * passages, width), F32),
             pltpu.VMEM((2 * passages, width), BF16),
             pltpu.VMEM((devices, 2 * passages, width), BF16),
-            pltpu.VMEM((2, chips, passages, 1, terms), F32),
-            pltpu.VMEM((chips, passages, 1, terms), F32),
-            dma((6,)),
+            pltpu.VMEM((chips * passages, terms), F32),
+            pltpu.VMEM((2, chips * passages, terms), F32),
+            dma((7,)),
             dma((chunks, chips + 1)),
             dma((chunks, chips + 1)),
             dma((devices,)),
@@ -454,35 +490,19 @@
         ),
     )(
         lengths,
+        cluster_ids,
         hidden,
         head_gain[None, :],
-        meta,
+        block_list,
+        vocab_bias[None, :],
         attn_weight,
         out_weight,
         up_weight,
         down_weight,
         head_weight,
         vocab_weight,
-    )
-    raw = pool.reshape(n * passages, terms)
-    mine = lax.dynamic_slice_in_dim(dall, grp * n, n, 0)[:, passages:]
-    flags = lax.dynamic_slice_in_dim(mine, term * (terms // BLOCK), terms // BLOCK, 2)
-    flags = flags.reshape(n * passages, terms // BLOCK)
-    value = jnp.log1p(jax.nn.relu(raw + vocab_bias.astype(F32)[None, :]))
-    keep = jnp.repeat(flags, BLOCK, axis=1) > 0.5
-    sparse = jnp.where(keep, value, 0.0).astype(BF16)
-    ids = dall[:, passages:, blocks : blocks + 2].astype(jnp.int32)
-    clusters = (ids[:, :, 0] * 256 + ids[:, :, 1]).reshape(devices * passages)
-    dense_rows = dall[:, :passages].reshape(devices * passages, width)
-    dense_part, slot_part = place_rows(
-        dense_rows,
-        jnp.arange(devices * passages, dtype=jnp.int32),
-        clusters,
-        clusters // CL_DEV == me,
         centroids,
-        me,
-    )
-    return (sparse, dense_part[None, :, :], slot_part[None, :])
+    )
 
 
 def solution(mesh):

time: 68.5 us -> 61.2 us (0.89)
  other arithmetic: 7.36 us -> 0 us
  local copies, waits for them, and re-layouts: 3.67 us -> 6.61 us
  Pallas kernels: 55.3 us -> 53.6 us
  matrix products: 1.01 us -> 0 us
    unnamed x4 -> x3, local copies, waits for them, and re-layouts: 0.01 us -> 4.05 us
    convert_element_type x5 -> x0, other arithmetic: 1.72 us -> none  [the longest x1 0.87 us: body(): ids = dall[:, passages:, blocks:blocks + 2].astype(jnp.int32)]
    pallas_call x1, Pallas kernels: 55.3 us -> 53.6 us  [body(): pl.pallas_call(functools.partial(kernel, groups, n, side, seq, chunk_pass...]
    pallas_call x1 -> x0, other arithmetic: 1.64 us -> none  [body(): pl.pallas_call(functools.partial(kernel, groups, n, side, seq, chunk_pass...]
    slice x1 -> x0, local copies, waits for them, and re-layouts: 1.05 us -> none  [body(): dense_rows = dall[:, :passages].reshape(devices * passages, width)]
    dot_general x2 -> x0, matrix products: 1.01 us -> none  [the longest x1 0.87 us: place_rows(): chosen = jnp.dot(lookup.astype(BF16), centroids, preferred_element_type=F32)]
    broadcast_in_dim x4 -> x1, local copies, waits for them, and re-layouts: 0.32 us -> 1.29 us  [body(): vocab_bias[None, :]]
    gt x2 -> x0, other arithmetic: 0.82 us -> none  [the longest x1 0.81 us: body(): keep = jnp.repeat(flags, BLOCK, axis=1) > 0.5]
where the time goes in v1:
time: 61.2 us; the launch traced here: 60.9 us
  Pallas kernels  53.6 us (88%)
  local copies, waits for them, and re-layouts  6.61 us (11%)
  between operations  0.64 us (1%)
    pallas_call x1, Pallas kernels, body(): pl.pallas_call(functools.partial(kernel, groups, n, side, seq, chunk_pass...  53.6 us
    unnamed x3, local copies, waits for them, and re-layouts  4.05 us
    broadcast_in_dim x1, local copies, waits for them, and re-layouts, body(): vocab_bias[None, :]  1.29 us
    broadcast_in_dim x1, local copies, waits for them, and re-layouts, body(): head_gain[None, :]  1.27 us

profile of v1, /device:TPU:0, one launch (start us, length us, event | category | flops | bytes accessed | tf_op | source)
XLA Modules:
  0.0 60.9 jit_solution(765163624602381001)
XLA Ops:
  0.6 1.3 %broadcast_in_dim.6.gain_ref = f32[1,768]{1,0:T(1,128)} reshape(f32[768]{0:T(1024)} %param.22) | data formatting | bytes 6144 | tf_op jit(solution)/shard_map/broadcast_in_dim | solution.py:495
  1.9 1.3 %broadcast_in_dim.7.bias_ref = bf16[1,2048]{1,0:T(2,128)(2,1)} reshape(bf16[2048]{0:T(1024)(128)(2,1)} %param.24) | data formatting | bytes 8192 | tf_op jit(solution)/shard_map/broadcast_in_dim | solution.py:497
  3.2 53.6 %shard_map.148 = (bf16[32,2048]{1,0:T(8,128)(2,1)}, bf16[1,16,768]{2,1,0:T(8,128)(2,1)}, s32[1,16]{1,0:T(1,128)}) custom-call(s32[4]{0:T(128)} %len_ref.1, s32[4]{0:T(128)} %cid_ref.1, bf16[512,768]{1,0:T(8,128)(2,1)} %hid_ref.1, f32[1,768]{1,0:T(1,128)} %broadcast_in_dim.6.gain_ref, s32[4,96]{1,0:T(4,128)} %blk_ref.1, ...), custom_call_target="tpu_custom_call" | custom-call | tf_op jit(solution)/shard_map/pallas_call | solution.py:453
  56.8 1.6 %copy.19 = bf16[32,2048]{1,0:T(8,128)(2,1)} copy(bf16[32,2048]{1,0:T(8,128)(2,1)} %get-tuple-element.6) | data formatting | bytes 262144
  58.4 1.3 %copy.20 = bf16[1,16,768]{2,1,0:T(8,128)(2,1)} copy(bf16[1,16,768]{2,1,0:T(8,128)(2,1)} %get-tuple-element.7) | data formatting | bytes 49152
  59.7 1.1 %copy.21 = s32[1,16]{1,0:T(1,128)} copy(s32[1,16]{1,0:T(1,128)} %get-tuple-element.8) | data formatting | bytes 128

commit v2 on v1

--- a/solution.py
+++ b/solution.py
@@ -226,6 +226,11 @@
             cols = slice(c * width, (c + 1) * width)
             joined[:, cols] = mm(x, aw[:, cols]).astype(BF16)
 
+        @pl.when(h == 0)
+        def _():
+            pl.semaphore_wait(barrier, devices - 1)
+            voc_copy.start()
+
         def attend(p, carry):
             span = pl.ds(pl.multiple_of(p * seq, seq), seq)
             live = key_place < len_ref[h * chunk_passages + p]
@@ -248,7 +253,7 @@
         first_wait(h, 1)
         fst[...] = norm(x.astype(F32) + mm(ctx[...], ow[...])).astype(BF16)
         first_wait(h, 2)
-        tile = 512
+        tile = 1536
 
         def up(j, carry):
             cols = pl.ds(pl.multiple_of(j * tile, tile), tile)
@@ -262,16 +267,11 @@
         for p in range(chunk_passages):
             dacc[pl.ds(h * chunk_passages + p, 1), :] = wide[p * seq : p * seq + 1]
         first_wait(h, 4)
-        out = norm(gelu(mm(layer_out, hw[...]))) * gain_ref[...]
+        out = norm(gelu(mm(layer_out, hw[...]))) * gain_ref[...][None, :]
         for p in range(chunk_passages):
             one = out[p * seq : (p + 1) * seq]
             one = jnp.where(row_place < len_ref[h * chunk_passages + p], one, one[0:1])
             gath[0, h, p * seq : (p + 1) * seq, :] = one.astype(BF16)
-
-        @pl.when(h == 0)
-        def _():
-            pl.semaphore_wait(barrier, devices - 1)
-            voc_copy.start()
 
         @pl.when(h > 0)
         def _():
@@ -292,53 +292,69 @@
         return carry
 
     lax.fori_loop(0, chunks, encode, 0)
+    terms = voc_hbm.shape[0]
+    tile = min(2048, terms)
+    per_part = terms // tile
+
+    def score(h, k, parts=(1, 0)):
+        c = source(k)
+        for part in parts:
+            for j in range(per_part):
+                cols = slice(j * tile, (j + 1) * tile)
+                logits = mm_nt(gath[k, h], voc[part, cols, :])
+                for p in range(chunk_passages):
+                    best = jnp.max(logits[p * seq : (p + 1) * seq], axis=0, keepdims=True)
+                    row = pl.ds(c * passages + h * chunk_passages + p, 1)
+                    if part == 0:
+                        res[core, row, cols] = best
+                    else:
+                        pool[row, cols] = best
+
     loads[5].wait()
+
+    @pl.loop(0, chunks)
+    def _(h):
+        score(h, 0, (0,))
+
     voc_copy.wait_recv()
 
-    terms = voc_hbm.shape[0]
-    tile = min(1024, terms)
-    per_part = terms // tile
-
-    def score(h, k):
-        c = source(k)
-
-        def step(j, carry):
-            part, at = j // per_part, pl.multiple_of((j % per_part) * tile, tile)
-            logits = mm_nt(gath[k, h], voc[part, pl.ds(at, tile), :])
-            for p in range(chunk_passages):
-                best = jnp.max(logits[p * seq : (p + 1) * seq], axis=0, keepdims=True)
-                row = pl.ds(c * passages + h * chunk_passages + p, 1)
-
-                @pl.when(part == 0)
-                def _():
-                    res[core, row, pl.ds(at, tile)] = best
-
-                @pl.when(part == 1)
-                def _():
-                    pool[row, pl.ds(at, tile)] = best
-            return carry
-
-        lax.fori_loop(0, 2 * per_part, step, 0)
-
-    for h in range(chunks):
-        score(h, 0)
-    for h in range(chunks):
-        if relay:
-            if h == chunks - 1:
-                send_relay(h)
-            score(h, 1)
-            score(h, 2)
+    @pl.loop(0, chunks)
+    def _(h):
+        score(h, 0, (1,))
+
+    if relay:
+        last = chunks - 1
+
+        @pl.loop(0, 2 * chunks)
+        def _(i):
+            @pl.when(i == 2 * last)
+            def _():
+                send_relay(last)
+
+            score(i // 2, 1 + i % 2)
+
+        @pl.loop(0, chunks)
+        def _(h):
             relay_copy(h, 0).wait_recv()
             relay_copy(h, 1).wait_recv()
-            score(h, 3)
-        else:
-
+            score(h, 3, (1,))
+
+        pool_copy.start()
+
+        @pl.loop(0, chunks)
+        def _(h):
+            score(h, 3, (0,))
+    else:
+
+        @pl.loop(0, chunks)
+        def _(h):
             @pl.loop(1, chips)
             def _(k):
                 tok_copy(h, k).wait_recv()
                 score(h, k)
 
-    pool_copy.start()
+        pool_copy.start()
+
     dall[me] = payload[...]
 
     @pl.loop(1, devices)
@@ -396,7 +412,7 @@
     both = []
     for c in range(chips):
         both += [res[s, c * passages : (c + 1) * passages] for s in range(2)]
-    raw = jnp.concatenate(both, axis=0) + bias_ref[...].astype(F32)
+    raw = jnp.concatenate(both, axis=0) + bias_ref[...].astype(F32)[None, :]
     sparse_out[...] = jnp.where(keep, jnp.log1p(jnp.maximum(raw, 0.0)), 0.0).astype(BF16)
 
     pool_copy.wait_send()
@@ -492,9 +508,9 @@
         lengths,
         cluster_ids,
         hidden,
-        head_gain[None, :],
+        head_gain,
         block_list,
-        vocab_bias[None, :],
+        vocab_bias,
         attn_weight,
         out_weight,
         up_weight,

time: 61.2 us -> 59.4 us (0.971)
  local copies, waits for them, and re-layouts: 6.61 us -> 4.05 us
  Pallas kernels: 53.6 us -> 54.5 us
    broadcast_in_dim x2 -> x0, local copies, waits for them, and re-layouts: 2.56 us -> none  [the longest x1 1.29 us: body(): vocab_bias[None, :]]
    pallas_call x1, Pallas kernels: 53.6 us -> 54.5 us  [body(): pl.pallas_call(functools.partial(kernel, groups, n, side, seq, chunk_pass...]
where the time goes in v2:
time: 59.4 us; the launch traced here: 59.2 us
  Pallas kernels  54.5 us (92%)
  local copies, waits for them, and re-layouts  4.05 us (7%)
  between operations  0.64 us (1%)
    pallas_call x1, Pallas kernels, body(): pl.pallas_call(functools.partial(kernel, groups, n, side, seq, chunk_pass...  54.5 us
    unnamed x3, local copies, waits for them, and re-layouts  4.05 us

profile of v2, /device:TPU:0, one launch (start us, length us, event | category | flops | bytes accessed | tf_op | source)
XLA Modules:
  0.0 59.2 jit_solution(14650722451997305394)
XLA Ops:
  0.6 54.5 %shard_map.148 = (bf16[32,2048]{1,0:T(8,128)(2,1)}, bf16[1,16,768]{2,1,0:T(8,128)(2,1)}, s32[1,16]{1,0:T(1,128)}) custom-call(s32[4]{0:T(128)} %len_ref.1, s32[4]{0:T(128)} %cid_ref.1, bf16[512,768]{1,0:T(8,128)(2,1)} %hid_ref.1, f32[768]{0:T(1024)} %gain_ref.1, s32[4,96]{1,0:T(4,128)} %blk_ref.1, bf16[2048]{0:T(1024)(128)(2,1)} %bias_ref.1, ...), custom_call_target="tpu_custom_call" | custom-call | tf_op jit(solution)/shard_map/pallas_call | solution.py:469
  55.1 1.6 %copy.19 = bf16[32,2048]{1,0:T(8,128)(2,1)} copy(bf16[32,2048]{1,0:T(8,128)(2,1)} %get-tuple-element.6) | data formatting | bytes 262144
  56.7 1.3 %copy.20 = bf16[1,16,768]{2,1,0:T(8,128)(2,1)} copy(bf16[1,16,768]{2,1,0:T(8,128)(2,1)} %get-tuple-element.7) | data formatting | bytes 49152
  58.0 1.1 %copy.21 = s32[1,16]{1,0:T(1,128)} copy(s32[1,16]{1,0:T(1,128)} %get-tuple-element.8) | data formatting | bytes 128
